TPU v7x, 32 devices: a whole 2x2x4 slice. The times are simulated.
32 devices in a mesh: grp: 2 (over y), row: 4 (over z), col: 2 (over x), slc: 2 (over core).
Axes of the slice: x: 2, y: 2, z: 4, core: 2. Of those that a mesh axis runs over, the one named last changes fastest.
Arguments:
- objects: bfloat16 [2, 2, 3072, 768], P(None, None, ('grp', 'row'), 'col'), parts along dimension 2, may hold values from -1 to 1
- probes: bfloat16 [4, 2, 256, 256], P(('grp', 'slc')), parts along dimension 0, may hold values from -3 to 3
- weights: float32 [256, 256], replicated, may hold values from 0.1 to 1
- counts: int32 [8, 2], P(('grp', 'row'), 'col'), parts along dimension 0, may hold values from 1 to 2, as said below
- offsets: int32 [8, 2, 2, 2], P(('grp', 'row'), 'col'), parts along dimension 0, may hold values from 0 to 383, as said below
- intensities: bfloat16 [8, 2, 2, 256, 256], P(('grp', 'row'), 'col'), parts along dimension 0, may hold values from 0.049804688 to 2
Outputs:
- gradient: float32 [2, 2, 3072, 768], P('slc', None, ('grp', 'row'), 'col'), parts along dimension 2
There are 2 independent parts, one for each index of `grp`. A program takes and returns all parts, laid end to end along the dimension named above; an argument that names none is the same for every part. Nothing has to cross between parts.
Inputs may be any that keep to these rules, and one draw needn't show every extreme that they name: `counts`: some tile has exactly 2 positions. `offsets`: every window of a live position lies inside the object; entries of slots at or after a tile's count are ignored.
All inputs are finite; a program needn't handle non-finite values.
Results may differ from a plain program's by a relative error of at most 0.019.
Values may be sent and summed in bfloat16 or wider, within the bound.
A program may use at most 64 MiB of HBM per device.

v0:
```python
import jax
import jax.numpy as jnp
from jax import lax
from jax.sharding import PartitionSpec as P

fresnel = 0.5


def from_behind(x, axis, by):
    count = lax.axis_size(axis)
    pairs = [(i, i + by) for i in range(count) if 0 <= i + by < count]
    return lax.ppermute(x, axis, pairs)


def dft_tables(extent):
    counter = jnp.arange(extent, dtype=jnp.int32)
    product = counter[:, None] * counter[None, :] % extent
    angles = 2.0 * jnp.pi / extent * product.astype(jnp.float32)
    norm_scale = 1.0 / jnp.sqrt(jnp.asarray(extent, jnp.float32))
    table_re = (jnp.cos(angles) * norm_scale).astype(jnp.bfloat16)
    table_im = (-jnp.sin(angles) * norm_scale).astype(jnp.bfloat16)
    return (table_re, table_im)


def chirp_factor(extent):
    counter = jnp.arange(extent, dtype=jnp.int32)
    signed_freq = (counter + extent // 2) % extent - extent // 2
    squares = (
        signed_freq[:, None] * signed_freq[:, None] + signed_freq[None, :] * signed_freq[None, :]
    )
    angles = -jnp.pi * fresnel / extent * squares.astype(jnp.float32)
    return (jnp.cos(angles), jnp.sin(angles))


def transform(real, imag, table_re, table_im):
    real_half = real.astype(jnp.bfloat16)
    imag_half = imag.astype(jnp.bfloat16)
    mid_re = jnp.dot(table_re, real_half, preferred_element_type=jnp.float32) - jnp.dot(
        table_im, imag_half, preferred_element_type=jnp.float32
    )
    mid_im = jnp.dot(table_re, imag_half, preferred_element_type=jnp.float32) + jnp.dot(
        table_im, real_half, preferred_element_type=jnp.float32
    )
    mid_re = mid_re.astype(jnp.bfloat16)
    mid_im = mid_im.astype(jnp.bfloat16)
    out_re = jnp.dot(mid_re, table_re, preferred_element_type=jnp.float32) - jnp.dot(
        mid_im, table_im, preferred_element_type=jnp.float32
    )
    out_im = jnp.dot(mid_re, table_im, preferred_element_type=jnp.float32) + jnp.dot(
        mid_im, table_re, preferred_element_type=jnp.float32
    )
    return (out_re, out_im)


def complex_mul(left_re, left_im, right_re, right_im):
    return (left_re * right_re - left_im * right_im, left_re * right_im + left_im * right_re)


def conj_mul(left_re, left_im, right_re, right_im):
    return (left_re * right_re + left_im * right_im, left_re * right_im - left_im * right_re)


def forward_mode(probe_re, probe_im, window, tables, chirps):
    table_re, table_im, inverse_im = tables
    chirp_re, chirp_im = chirps
    first_re = window[0, 0].astype(jnp.float32)
    first_im = window[0, 1].astype(jnp.float32)
    second_re = window[1, 0].astype(jnp.float32)
    second_im = window[1, 1].astype(jnp.float32)
    psi_re, psi_im = complex_mul(probe_re, probe_im, first_re, first_im)
    spec_re, spec_im = transform(psi_re, psi_im, table_re, table_im)
    spec_re, spec_im = complex_mul(chirp_re, chirp_im, spec_re, spec_im)
    prop_re, prop_im = transform(spec_re, spec_im, table_re, inverse_im)
    exit_re, exit_im = complex_mul(prop_re, prop_im, second_re, second_im)
    far_re, far_im = transform(exit_re, exit_im, table_re, table_im)
    return (prop_re, prop_im, far_re, far_im)


def backward_mode(
    probe_re, probe_im, window, prop_re, prop_im, far_re, far_im, residual, tables, chirps
):
    table_re, table_im, inverse_im = tables
    chirp_re, chirp_im = chirps
    second_re = window[1, 0].astype(jnp.float32)
    second_im = window[1, 1].astype(jnp.float32)
    back_re, back_im = transform(residual * far_re, residual * far_im, table_re, inverse_im)
    grad_two_re, grad_two_im = conj_mul(prop_re, prop_im, back_re, back_im)
    gprop_re, gprop_im = conj_mul(second_re, second_im, back_re, back_im)
    gspec_re, gspec_im = transform(gprop_re, gprop_im, table_re, table_im)
    gspec_re, gspec_im = conj_mul(chirp_re, chirp_im, gspec_re, gspec_im)
    gpsi_re, gpsi_im = transform(gspec_re, gspec_im, table_re, inverse_im)
    grad_one_re, grad_one_im = conj_mul(probe_re, probe_im, gpsi_re, gpsi_im)
    return jnp.stack([jnp.stack([grad_one_re, grad_one_im]), jnp.stack([grad_two_re, grad_two_im])])


def body(objects, probes, weights, counts, offsets, intensities):
    slices = objects.shape[0]
    tile_size = objects.shape[2]
    extent = probes.shape[2]
    table_re, table_im = dft_tables(extent)
    tables = (table_re, table_im, -table_im)
    chirps = chirp_factor(extent)
    probe_re = probes[0, 0].astype(jnp.float32)
    probe_im = probes[0, 1].astype(jnp.float32)
    from_right = from_behind(objects[:, :, :, :extent], "col", -1)
    widened = jnp.concatenate([objects, from_right], axis=3)
    from_below = from_behind(widened[:, :, :extent, :], "row", -1)
    extended = jnp.concatenate([widened, from_below], axis=2)
    tile_count = counts[0, 0]
    offset_list = offsets[0, 0]
    measured = intensities[0, 0]
    slot_limit = offset_list.shape[0]
    anchor = jnp.int32(0)

    def slot_gradient(window, data_slot):
        prop_re, prop_im, far_re, far_im = forward_mode(probe_re, probe_im, window, tables, chirps)
        intensity = lax.psum(
            (far_re * far_re + far_im * far_im).astype(jnp.bfloat16), "slc"
        ).astype(jnp.float32)
        residual = 2.0 * weights * (intensity - data_slot.astype(jnp.float32))
        return backward_mode(
            probe_re, probe_im, window, prop_re, prop_im, far_re, far_im, residual, tables, chirps
        )

    def window_at(slot_id):
        corner = offset_list[slot_id]
        return lax.dynamic_slice(
            extended, (anchor, anchor, corner[0], corner[1]), (slices, 2, extent, extent)
        )

    def add_at(gradient, slot_id, contrib):
        corner = offset_list[slot_id]
        start = (anchor, anchor, corner[0], corner[1])
        previous = lax.dynamic_slice(gradient, start, (slices, 2, extent, extent))
        return lax.dynamic_update_slice(gradient, previous + contrib, start)

    gradient = jnp.zeros(extended.shape, jnp.float32)

    def own_step(slot_id, gradient_now):
        contrib = slot_gradient(window_at(slot_id), measured[slot_id])
        contrib = jnp.where(slot_id < tile_count, contrib, jnp.zeros_like(contrib))
        return add_at(gradient_now, slot_id, contrib)

    gradient = lax.fori_loop(0, slot_limit, own_step, gradient)
    share = lax.psum_scatter(
        gradient.astype(jnp.bfloat16), "slc", scatter_dimension=0, tiled=True
    ).astype(jnp.float32)
    from_above = from_behind(share[:, :, tile_size:, :].astype(jnp.bfloat16), "row", 1).astype(
        jnp.float32
    )
    share = jnp.concatenate(
        [share[:, :, :extent, :] + from_above, share[:, :, extent:tile_size, :]], axis=2
    )
    from_left = from_behind(share[:, :, :, tile_size:].astype(jnp.bfloat16), "col", 1).astype(
        jnp.float32
    )
    return jnp.concatenate(
        [share[:, :, :, :extent] + from_left, share[:, :, :, extent:tile_size]], axis=3
    )


def solution(mesh):
    in_specs = (
        P(None, None, ("grp", "row"), "col"),
        P(("grp", "slc"), None, None, None),
        P(),
        P(("grp", "row"), "col"),
        P(("grp", "row"), "col", None, None),
        P(("grp", "row"), "col", None, None, None),
    )
    out_specs = P("slc", None, ("grp", "row"), "col")
    return jax.shard_map(body, mesh=mesh, in_specs=in_specs, out_specs=out_specs, check_vma=False)
```

profile of v0, /device:TPU:10, one launch (start us, length us, event | category | flops | bytes accessed | tf_op | source)
XLA Modules:
  0.0 331.7 jit_solution(6804542011698405931)
XLA Ops:
  8.7 2.5 collective-permute-start
  11.3 16.6 %collective-permute-done = bf16[2,2,384,256]{3,2,1,0:T(8,128)(2,1)S(1)} collective-permute-done((bf16[2,2,384,256]{3,2,1,0:T(8,128)(2,1)S(1)}, bf16[2,2,384,256]{3,2,1,0:T(8,128)(2,1)S(1)}, u32[]{:S(2)}, u32[]{:S(2)}) %collective-permute-start) | collective-permute-done | bytes 786464 | tf_op jit(solution)/shard_map/ppermute | solution.py:12
  29.1 1.9 collective-permute-start.1
  31.1 29.9 %collective-permute-done.1 = bf16[2,2,256,640]{3,2,1,0:T(8,128)(2,1)} collective-permute-done((bf16[2,2,256,640]{3,2,1,0:T(8,128)(2,1)}, bf16[2,2,256,640]{3,2,1,0:T(8,128)(2,1)}, u32[]{:S(2)}, u32[]{:S(2)}) %collective-permute-start.1) | collective-permute-done | bytes 1310752 | tf_op jit(solution)/shard_map/ppermute | solution.py:12
  61.0 3.3 %pad_maximum_fusion = bf16[2,2,640,640]{3,2,1,0:T(8,128)(2,1)} fusion(bf16[2,2,256,640]{3,2,1,0:T(8,128)(2,1)} %collective-permute-done.1, bf16[2,2,384,640]{3,2,1,0:T(8,128)(2,1)S(1)} %constant_dynamic-update-slice_fusion), kind=kLoop, calls=%fused_computation.378 | loop fusion | flops 6553600 | bytes 6553600 | tf_op jit(solution)/shard_map/concatenate | solution.py:108
  64.3 3.1 broadcast_in_dim.2
  67.5 205.5 %while.16 = (s32[]{:T(128)}, f32[2,2,640,640]{3,2,1,0:T(8,128)}, s32[2,2]{1,0:T(2,128)S(1)}, s32[]{:T(128)}, bf16[2,2,640,640]{3,2,1,0:T(8,128)(2,1)}, /*index=5...) while((s32[]{:T(128)}, f32[2,2,640,640]{3,2,1,0:T(8,128)}, ...), condition=%wide.region_2.3_spmd.clone.clone.clone, body=%wide.region_0.2_spmd.clone.clone.clone.sunk | while | flops 1673396224 | bytes 38406500 | solution.py:144
  81.6 2.0 fusion.569
  85.9 1.7 fusion.571
  92.3 2.2 fusion.576
  102.7 1.8 add_convert_fusion.2
  105.2 18.9 %all-reduce.2.cloned.1.call-done = bf16[256,256]{1,0:T(8,128)(2,1)} async-done(((bf16[256,256]{1,0:T(8,128)(2,1)}), bf16[256,256]{1,0:T(8,128)(2,1)}) %all-reduce.2.cloned.1.call-update) | async-done | bytes 131088 | tf_op jit(solution)/shard_map/while/body/eval_jaxpr/psum | solution.py:117
  133.0 2.5 fusion.589
  143.6 2.0 fusion.596
  147.9 1.5 fusion.598
  155.3 1.8 fusion.603
  157.2 12.0 %dynamic_update_slice.11 = f32[2,2,640,640]{3,2,1,0:T(8,128)} dynamic-update-slice(f32[2,2,640,640]{3,2,1,0:T(8,128)} %get-tuple-element.705, f32[2,2,256,256]{3,2,1,0:T(8,128)S(1)} %fusion.603, s32[]{:T(128)} %constant.69.clone.1..sunk, s32[]{:T(128)} %constant.69.clone.1..sunk, s32[]{:T(128)S(6)} %select_n.381, s32[]{:T(128)S(6)} %select_n.382) | dynamic-update-slice | bytes 2097156 | tf_op jit(solution)/shard_map/while/body/eval_jaxpr/dynamic_update_slice | solution.py:135
  183.2 2.0 fusion.569
  187.6 1.5 fusion.571
  193.7 2.2 fusion.576
  204.2 1.8 add_convert_fusion.2
  206.6 19.0 %all-reduce.2.cloned.1.call-done = bf16[256,256]{1,0:T(8,128)(2,1)} async-done(((bf16[256,256]{1,0:T(8,128)(2,1)}), bf16[256,256]{1,0:T(8,128)(2,1)}) %all-reduce.2.cloned.1.call-update) | async-done | bytes 131088 | tf_op jit(solution)/shard_map/while/body/eval_jaxpr/psum | solution.py:117
  234.6 2.5 fusion.589
  245.2 2.0 fusion.596
  249.5 1.5 fusion.598
  256.9 1.8 fusion.603
  258.7 12.3 %dynamic_update_slice.11 = f32[2,2,640,640]{3,2,1,0:T(8,128)} dynamic-update-slice(f32[2,2,640,640]{3,2,1,0:T(8,128)} %get-tuple-element.705, f32[2,2,256,256]{3,2,1,0:T(8,128)S(1)} %fusion.603, s32[]{:T(128)} %constant.69.clone.1..sunk, s32[]{:T(128)} %constant.69.clone.1..sunk, s32[]{:T(128)S(6)} %select_n.381, s32[]{:T(128)S(6)} %select_n.382) | dynamic-update-slice | bytes 2097156 | tf_op jit(solution)/shard_map/while/body/eval_jaxpr/dynamic_update_slice | solution.py:135
  273.0 4.9 %convert_element_type.492 = bf16[2,2,640,640]{3,2,1,0:T(8,128)(2,1)} convert(f32[2,2,640,640]{3,2,1,0:T(8,128)} %get-tuple-element.387) | non-fusion elementwise | flops 1638400 | bytes 9830400 | tf_op jit(solution)/shard_map/convert_element_type | solution.py:146
  278.0 12.6 %reduce-scatter.2.cloned.1.call-done = bf16[1,2,640,640]{3,2,1,0:T(8,128)(2,1)} async-done(((bf16[2,2,640,640]{3,2,1,0:T(8,128)(2,1)}), bf16[1,2,640,640]{3,2,1,0:T(8,128)(2,1)}) %reduce-scatter.2.cloned.1.call-update) | async-done | bytes 1638416 | tf_op jit(solution)/shard_map/reduce_scatter | solution.py:145
  291.9 3.4 %collective-permute-start.2 = (bf16[1,2,256,640]{3,2,1,0:T(8,128)(2,1)S(1)}, bf16[1,2,256,640]{3,2,1,0:T(8,128)(2,1)S(1)}, u32[]{:S(2)}, u32[]{:S(2)}) collective-permute-start(bf16[1,2,256,640]{3,2,1,0:T(8,128)(2,1)S(1)} %slice.110), channel_id=1, source_target_pairs={{0,4},{4,8},{8,12},{1,5},{5,9},{9,13},{2,6},{6,10},{10,14},{3,7},{... | collective-permute-start | bytes 1966088 | tf_op jit(solution)/shard_map/ppermute | solution.py:12
  296.6 14.0 %collective-permute-done.2 = bf16[1,2,256,640]{3,2,1,0:T(8,128)(2,1)S(1)} collective-permute-done((bf16[1,2,256,640]{3,2,1,0:T(8,128)(2,1)S(1)}, bf16[1,2,256,640]{3,2,1,0:T(8,128)(2,1)S(1)}, u32[]{:S(2)}, u32[]{:S(2)}) %collective-permute-start.2) | collective-permute-done | bytes 655392 | tf_op jit(solution)/shard_map/ppermute | solution.py:12
  312.0 10.9 %collective-permute-done.3 = bf16[1,2,384,256]{3,2,1,0:T(8,128)(2,1)S(1)} collective-permute-done((bf16[1,2,384,256]{3,2,1,0:T(8,128)(2,1)S(1)}, bf16[1,2,384,256]{3,2,1,0:T(8,128)(2,1)S(1)}, u32[]{:S(2)}, u32[]{:S(2)}) %collective-permute-start.3) | collective-permute-done | bytes 393248 | tf_op jit(solution)/shard_map/ppermute | solution.py:12
  (124 shorter events, 107.5 us)
Async XLA Ops:
  7.4 3.8 %copy-start.2 = (bf16[2,2,384,384]{3,2,1,0:T(8,128)(2,1)S(1)}, bf16[2,2,384,384]{3,2,1,0:T(8,128)(2,1)}, u32[]{:S(2)}) copy-start(bf16[2,2,384,384]{3,2,1,0:T(8,128)(2,1)} %param.8) | copy-start | bytes 3538948
  8.7 19.2 %collective-permute-start = (bf16[2,2,384,256]{3,2,1,0:T(8,128)(2,1)S(1)}, bf16[2,2,384,256]{3,2,1,0:T(8,128)(2,1)S(1)}, u32[]{:S(2)}, u32[]{:S(2)}) collective-permute-start(bf16[2,2,384,256]{3,2,1,0:T(8,128)(2,1)S(1)} %slice.80), channel_id=1, source_target_pairs={{2,0},{3,1},{6,4},{7,5},{10,8},{11,9},{14,12},{15,13},{18,16},{19,... | collective-permute-start | bytes 2359304 | tf_op jit(solution)/shard_map/ppermute | solution.py:12
  11.3 19.8 %copy-start.4 = (bf16[1,2,256,256]{3,2,1,0:T(8,128)(2,1)S(1)}, bf16[1,2,256,256]{3,2,1,0:T(8,128)(2,1)}, u32[]{:S(2)}) copy-start(bf16[1,2,256,256]{3,2,1,0:T(8,128)(2,1)} %param.9) | copy-start | bytes 786436
  29.1 31.9 %collective-permute-start.1 = (bf16[2,2,256,640]{3,2,1,0:T(8,128)(2,1)}, bf16[2,2,256,640]{3,2,1,0:T(8,128)(2,1)}, u32[]{:S(2)}, u32[]{:S(2)}) collective-permute-start(bf16[2,2,256,640]{3,2,1,0:T(8,128)(2,1)} %slice.108), channel_id=1, source_target_pairs={{4,0},{8,4},{12,8},{5,1},{9,5},{13,9},{6,2},{10,6},{14,10},{7,3},{... | collective-permute-start | bytes 3932168 | tf_op jit(solution)/shard_map/ppermute | solution.py:12
  64.3 3.1 copy-start
  64.3 3.1 copy-start.3
  64.3 3.1 copy-start.5
  67.7 56.4 %all-reduce.2.cloned.1.call-start = ((), (), s32[]{:S(2)}) async-start(), calls=%async_computation.2 | async-start | bytes 262144 | tf_op jit(solution)/shard_map/while/body/eval_jaxpr/psum | solution.py:117
  169.3 56.3 %all-reduce.2.cloned.1.call-start = ((), (), s32[]{:S(2)}) async-start(), calls=%async_computation.2 | async-start | bytes 262144 | tf_op jit(solution)/shard_map/while/body/eval_jaxpr/psum | solution.py:117
  273.0 17.7 %reduce-scatter.2.cloned.1.call-start = ((), (), s32[]{:S(2)}) async-start(), calls=%async_computation.1 | async-start | bytes 4915200 | tf_op jit(solution)/shard_map/reduce_scatter | solution.py:145
  290.6 5.7 %copy-start.1 = (bf16[1,2,640,640]{3,2,1,0:T(8,128)(2,1)S(1)}, bf16[1,2,640,640]{3,2,1,0:T(8,128)(2,1)}, u32[]{:S(2)}) copy-start(bf16[1,2,640,640]{3,2,1,0:T(8,128)(2,1)} %reduce-scatter.2.cloned.1.call-done) | copy-start | bytes 4915204
  291.9 18.6 %collective-permute-start.2 = (bf16[1,2,256,640]{3,2,1,0:T(8,128)(2,1)S(1)}, bf16[1,2,256,640]{3,2,1,0:T(8,128)(2,1)S(1)}, u32[]{:S(2)}, u32[]{:S(2)}) collective-permute-start(bf16[1,2,256,640]{3,2,1,0:T(8,128)(2,1)S(1)} %slice.110), channel_id=1, source_target_pairs={{0,4},{4,8},{8,12},{1,5},{5,9},{9,13},{2,6},{6,10},{10,14},{3,7},{... | collective-permute-start | bytes 1966088 | tf_op jit(solution)/shard_map/ppermute | solution.py:12
  310.7 12.2 %collective-permute-start.3 = (bf16[1,2,384,256]{3,2,1,0:T(8,128)(2,1)S(1)}, bf16[1,2,384,256]{3,2,1,0:T(8,128)(2,1)S(1)}, u32[]{:S(2)}, u32[]{:S(2)}) collective-permute-start(bf16[1,2,384,256]{3,2,1,0:T(8,128)(2,1)S(1)} %fusion.339), channel_id=1, source_target_pairs={{0,2},{1,3},{4,6},{5,7},{8,10},{9,11},{12,14},{13,15},{16,18},{17,... | collective-permute-start | bytes 1179656 | tf_op jit(solution)/shard_map/ppermute | solution.py:12
Sparse Core Ops, SparseCore 0:
  104.7 19.3 all-reduce.1
  206.1 19.4 all-reduce.1
Sparse Core Ops, SparseCore 1:
  278.1 12.5 reduce-scatter.1
where the time goes:
time: 335 us; the launch traced here: 332 us
  waiting for transfers between devices  122 us (36%)
  matrix products  121 us (36%)
  local copies, waits for them, and re-layouts  33.5 us (10%)
  other arithmetic  18.1 us (5%)
  between operations  15.2 us (5%)
  loops' own time  12.4 us (4%)
  starting transfers between devices  9.21 us (3%)
    ppermute x4, waiting for transfers between devices, from_behind(): return lax.ppermute(x, axis, pairs)  71.3 us
    psum x2, waiting for transfers between devices, slot_gradient(): lax.psum((far_re * far_re + far_im * far_im).astype(jnp.bfloat16), 'slc')  37.8 us
    dynamic_update_slice x2, local copies, waits for them, and re-layouts, add_at(): return lax.dynamic_update_slice(gradient, previous + contrib, start)  24.3 us
    dot_general x12, matrix products, transform(): jnp.dot(mid_im, table_im, preferred_element_type=jnp.float32)  20.2 us
    dot_general x12, matrix products, transform(): jnp.dot(mid_im, table_re, preferred_element_type=jnp.float32)  17.2 us
    dot_general x12, matrix products, transform(): jnp.dot(table_im, imag_half, preferred_element_type=jnp.float32)  15.5 us
    dot_general x12, matrix products, transform(): jnp.dot(table_im, real_half, preferred_element_type=jnp.float32)  14.1 us
    dot_general x12, matrix products, transform(): jnp.dot(mid_re, table_im, preferred_element_type=jnp.float32)  13.7 us
  transfers between devices with their start and end apart: 7, of which 7 were waited for; matrix products, arithmetic and copies ran while one was open for 0% of the time, Pallas kernels for 0%

commit v1 on v0

--- a/solution.py
+++ b/solution.py
@@ -114,8 +114,8 @@
 
     def slot_gradient(window, data_slot):
         prop_re, prop_im, far_re, far_im = forward_mode(probe_re, probe_im, window, tables, chirps)
-        intensity = lax.psum(
-            (far_re * far_re + far_im * far_im).astype(jnp.bfloat16), "slc"
+        intensity = jnp.sum(
+            lax.all_gather((far_re * far_re + far_im * far_im).astype(jnp.bfloat16), "slc"), axis=0
         ).astype(jnp.float32)
         residual = 2.0 * weights * (intensity - data_slot.astype(jnp.float32))
         return backward_mode(

time: 335 us -> 296 us (0.88)
  waiting for transfers between devices: 122 us -> 84.3 us
  blocking collectives: 0 us -> 3.99 us
    psum x2 -> x0, waiting for transfers between devices: 37.8 us -> none  [slot_gradient(): lax.psum((far_re * far_re + far_im * far_im).astype(jnp.bfloat16), 'slc')]
    all_gather x0 -> x2, blocking collectives: none -> 3.99 us  [slot_gradient(): lax.all_gather((far_re * far_re + far_im * far_im).astype(jnp.bfloat16),...]
  transfers between devices with their start and end apart: 7 -> 5, of which waited for: 7 -> 5; matrix products, arithmetic and copies ran while one was open for 0% -> 0% of each run, Pallas kernels for 0% -> 0%
where the time goes in v1:
time: 296 us; the launch traced here: 293 us
  matrix products  120 us (41%)
  waiting for transfers between devices  84.3 us (28%)
  local copies, waits for them, and re-layouts  33.5 us (11%)
  other arithmetic  16.3 us (6%)
  between operations  13.7 us (5%)
  loops' own time  12 us (4%)
  starting transfers between devices  9.1 us (3%)
  blocking collectives  3.99 us (1%)
    ppermute x4, waiting for transfers between devices, from_behind(): return lax.ppermute(x, axis, pairs)  71.4 us
    dynamic_update_slice x2, local copies, waits for them, and re-layouts, add_at(): return lax.dynamic_update_slice(gradient, previous + contrib, start)  24.2 us
    dot_general x12, matrix products, transform(): jnp.dot(mid_im, table_im, preferred_element_type=jnp.float32)  19.8 us
    dot_general x12, matrix products, transform(): jnp.dot(mid_im, table_re, preferred_element_type=jnp.float32)  15.9 us
    dot_general x12, matrix products, transform(): jnp.dot(table_im, imag_half, preferred_element_type=jnp.float32)  14.7 us
    dot_general x12, matrix products, transform(): jnp.dot(mid_re, table_im, preferred_element_type=jnp.float32)  14.5 us
    dot_general x12, matrix products, transform(): jnp.dot(mid_re, table_re, preferred_element_type=jnp.float32)  14 us
    dot_general x12, matrix products, transform(): jnp.dot(table_re, imag_half, preferred_element_type=jnp.float32)  13.9 us
  transfers between devices with their start and end apart: 5, of which 5 were waited for; matrix products, arithmetic and copies ran while one was open for 0% of the time, Pallas kernels for 0%

profile of v1, /device:TPU:10, one launch (start us, length us, event | category | flops | bytes accessed | tf_op | source)
XLA Modules:
  0.0 293.1 jit_solution(16464025155087942481)
XLA Ops:
  7.8 2.5 collective-permute-start
  10.5 16.6 %collective-permute-done = bf16[2,2,384,256]{3,2,1,0:T(8,128)(2,1)S(1)} collective-permute-done((bf16[2,2,384,256]{3,2,1,0:T(8,128)(2,1)S(1)}, bf16[2,2,384,256]{3,2,1,0:T(8,128)(2,1)S(1)}, u32[]{:S(2)}, u32[]{:S(2)}) %collective-permute-start) | collective-permute-done | bytes 786464 | tf_op jit(solution)/shard_map/ppermute | solution.py:12
  28.3 1.9 collective-permute-start.1
  30.3 29.9 %collective-permute-done.1 = bf16[2,2,256,640]{3,2,1,0:T(8,128)(2,1)} collective-permute-done((bf16[2,2,256,640]{3,2,1,0:T(8,128)(2,1)}, bf16[2,2,256,640]{3,2,1,0:T(8,128)(2,1)}, u32[]{:S(2)}, u32[]{:S(2)}) %collective-permute-start.1) | collective-permute-done | bytes 1310752 | tf_op jit(solution)/shard_map/ppermute | solution.py:12
  60.2 3.3 %pad_maximum_fusion = bf16[2,2,640,640]{3,2,1,0:T(8,128)(2,1)} fusion(bf16[2,2,256,640]{3,2,1,0:T(8,128)(2,1)} %collective-permute-done.1, bf16[2,2,384,640]{3,2,1,0:T(8,128)(2,1)S(1)} %constant_dynamic-update-slice_fusion), kind=kLoop, calls=%fused_computation.378 | loop fusion | flops 6553600 | bytes 6553600 | tf_op jit(solution)/shard_map/concatenate | solution.py:108
  63.5 3.1 %broadcast_in_dim.2 = f32[2,2,640,640]{3,2,1,0:T(8,128)} broadcast(f32[]{:T(128)} %constant.95.clone.1), dimensions={} | broadcast | bytes 6553604 | tf_op jit(solution)/shard_map/broadcast_in_dim | solution.py:137
  66.6 168.1 %while.18 = (s32[]{:T(128)}, f32[2,2,640,640]{3,2,1,0:T(8,128)}, s32[2,2]{1,0:T(2,128)S(1)}, s32[]{:T(128)}, bf16[2,2,640,640]{3,2,1,0:T(8,128)(2,1)}, /*index=5...) while((s32[]{:T(128)}, f32[2,2,640,640]{3,2,1,0:T(8,128)}, ...), condition=%wide.region_2.3_spmd.clone.clone.clone, body=%wide.region_0.2_spmd.clone.clone.clone.sunk | while | flops 1673396224 | bytes 38406472 | solution.py:144
  81.2 2.0 fusion.569
  84.4 1.7 fusion.571
  91.9 2.2 fusion.576
  103.5 2.0 all-gather.4
  113.6 2.3 fusion.589
  118.2 1.3 fusion.593
  124.2 2.0 fusion.596
  131.9 1.5 fusion.599
  135.9 1.8 fusion.603
  137.7 12.0 %dynamic_update_slice.14 = f32[2,2,640,640]{3,2,1,0:T(8,128)} dynamic-update-slice(f32[2,2,640,640]{3,2,1,0:T(8,128)} %get-tuple-element.807, f32[2,2,256,256]{3,2,1,0:T(8,128)S(1)} %fusion.603, s32[]{:T(128)} %constant.94.clone.1..sunk, s32[]{:T(128)} %constant.94.clone.1..sunk, s32[]{:T(128)S(6)} %select_n.396, s32[]{:T(128)S(6)} %select_n.397) | dynamic-update-slice | bytes 2097156 | tf_op jit(solution)/shard_map/while/body/eval_jaxpr/dynamic_update_slice | solution.py:135
  164.3 2.0 fusion.569
  167.4 1.5 fusion.571
  174.7 2.2 fusion.576
  186.3 2.0 all-gather.4
  196.5 2.3 fusion.589
  201.1 1.3 fusion.593
  207.0 2.0 fusion.596
  214.8 1.5 fusion.599
  218.8 1.8 fusion.603
  220.6 12.2 %dynamic_update_slice.14 = f32[2,2,640,640]{3,2,1,0:T(8,128)} dynamic-update-slice(f32[2,2,640,640]{3,2,1,0:T(8,128)} %get-tuple-element.807, f32[2,2,256,256]{3,2,1,0:T(8,128)S(1)} %fusion.603, s32[]{:T(128)} %constant.94.clone.1..sunk, s32[]{:T(128)} %constant.94.clone.1..sunk, s32[]{:T(128)S(6)} %select_n.396, s32[]{:T(128)S(6)} %select_n.397) | dynamic-update-slice | bytes 2097156 | tf_op jit(solution)/shard_map/while/body/eval_jaxpr/dynamic_update_slice | solution.py:135
  234.7 4.9 %convert_element_type.591 = bf16[2,2,640,640]{3,2,1,0:T(8,128)(2,1)} convert(f32[2,2,640,640]{3,2,1,0:T(8,128)} %get-tuple-element.488) | non-fusion elementwise | flops 1638400 | bytes 9830400 | tf_op jit(solution)/shard_map/convert_element_type | solution.py:146
  239.7 12.9 %reduce-scatter.2.cloned.1.call-done = bf16[1,2,640,640]{3,2,1,0:T(8,128)(2,1)} async-done(((bf16[2,2,640,640]{3,2,1,0:T(8,128)(2,1)}), bf16[1,2,640,640]{3,2,1,0:T(8,128)(2,1)}) %reduce-scatter.2.cloned.1.call-update) | async-done | bytes 1638416 | tf_op jit(solution)/shard_map/reduce_scatter | solution.py:145
  253.8 3.4 %collective-permute-start.2 = (bf16[1,2,256,640]{3,2,1,0:T(8,128)(2,1)S(1)}, bf16[1,2,256,640]{3,2,1,0:T(8,128)(2,1)S(1)}, u32[]{:S(2)}, u32[]{:S(2)}) collective-permute-start(bf16[1,2,256,640]{3,2,1,0:T(8,128)(2,1)S(1)} %slice.128), channel_id=1, source_target_pairs={{0,4},{4,8},{8,12},{1,5},{5,9},{9,13},{2,6},{6,10},{10,14},{3,7},{... | collective-permute-start | bytes 1966088 | tf_op jit(solution)/shard_map/ppermute | solution.py:12
  258.5 14.0 %collective-permute-done.2 = bf16[1,2,256,640]{3,2,1,0:T(8,128)(2,1)S(1)} collective-permute-done((bf16[1,2,256,640]{3,2,1,0:T(8,128)(2,1)S(1)}, bf16[1,2,256,640]{3,2,1,0:T(8,128)(2,1)S(1)}, u32[]{:S(2)}, u32[]{:S(2)}) %collective-permute-start.2) | collective-permute-done | bytes 655392 | tf_op jit(solution)/shard_map/ppermute | solution.py:12
  274.0 10.9 %collective-permute-done.3 = bf16[1,2,384,256]{3,2,1,0:T(8,128)(2,1)S(1)} collective-permute-done((bf16[1,2,384,256]{3,2,1,0:T(8,128)(2,1)S(1)}, bf16[1,2,384,256]{3,2,1,0:T(8,128)(2,1)S(1)}, u32[]{:S(2)}, u32[]{:S(2)}) %collective-permute-start.3) | collective-permute-done | bytes 393248 | tf_op jit(solution)/shard_map/ppermute | solution.py:12
  (122 shorter events, 105.8 us)
Async XLA Ops:
  6.5 246.0 %reduce-scatter.2.cloned.1.call-start = ((), (), s32[]{:S(2)}) async-start(), calls=%async_computation.1 | async-start | bytes 4915200 | tf_op jit(solution)/shard_map/reduce_scatter | solution.py:145
  6.5 3.8 %copy-start.2 = (bf16[2,2,384,384]{3,2,1,0:T(8,128)(2,1)S(1)}, bf16[2,2,384,384]{3,2,1,0:T(8,128)(2,1)}, u32[]{:S(2)}) copy-start(bf16[2,2,384,384]{3,2,1,0:T(8,128)(2,1)} %param.8) | copy-start | bytes 3538948
  7.8 19.2 %collective-permute-start = (bf16[2,2,384,256]{3,2,1,0:T(8,128)(2,1)S(1)}, bf16[2,2,384,256]{3,2,1,0:T(8,128)(2,1)S(1)}, u32[]{:S(2)}, u32[]{:S(2)}) collective-permute-start(bf16[2,2,384,256]{3,2,1,0:T(8,128)(2,1)S(1)} %slice.98), channel_id=1, source_target_pairs={{2,0},{3,1},{6,4},{7,5},{10,8},{11,9},{14,12},{15,13},{18,16},{19,... | collective-permute-start | bytes 2359304 | tf_op jit(solution)/shard_map/ppermute | solution.py:12
  10.5 19.8 %copy-start.4 = (bf16[1,2,256,256]{3,2,1,0:T(8,128)(2,1)S(1)}, bf16[1,2,256,256]{3,2,1,0:T(8,128)(2,1)}, u32[]{:S(2)}) copy-start(bf16[1,2,256,256]{3,2,1,0:T(8,128)(2,1)} %param.9) | copy-start | bytes 786436
  28.3 31.9 %collective-permute-start.1 = (bf16[2,2,256,640]{3,2,1,0:T(8,128)(2,1)}, bf16[2,2,256,640]{3,2,1,0:T(8,128)(2,1)}, u32[]{:S(2)}, u32[]{:S(2)}) collective-permute-start(bf16[2,2,256,640]{3,2,1,0:T(8,128)(2,1)} %slice.126), channel_id=1, source_target_pairs={{4,0},{8,4},{12,8},{5,1},{9,5},{13,9},{6,2},{10,6},{14,10},{7,3},{... | collective-permute-start | bytes 3932168 | tf_op jit(solution)/shard_map/ppermute | solution.py:12
  63.5 3.1 %copy-start = (f32[256,256]{1,0:T(8,128)S(1)}, f32[256,256]{1,0:T(8,128)}, u32[]{:S(2)}) copy-start(f32[256,256]{1,0:T(8,128)} %param.10) | copy-start | bytes 786436
  63.5 3.1 %copy-start.3 = (bf16[1,1,2,256,256]{4,3,2,1,0:T(8,128)(2,1)S(1)}, bf16[1,1,2,256,256]{4,3,2,1,0:T(8,128)(2,1)}, u32[]{:S(2)}) copy-start(bf16[1,1,2,256,256]{4,3,2,1,0:T(8,128)(2,1)} %param.13) | copy-start | bytes 786436
  63.5 3.1 %copy-start.5 = (s32[1,1,2,2]{3,2,1,0:T(2,128)S(1)}, s32[1,1,2,2]{3,2,1,0:T(2,128)}, u32[]{:S(2)}) copy-start(s32[1,1,2,2]{3,2,1,0:T(2,128)} %param.12) | copy-start | bytes 52
  252.5 5.7 %copy-start.1 = (bf16[1,2,640,640]{3,2,1,0:T(8,128)(2,1)S(1)}, bf16[1,2,640,640]{3,2,1,0:T(8,128)(2,1)}, u32[]{:S(2)}) copy-start(bf16[1,2,640,640]{3,2,1,0:T(8,128)(2,1)} %reduce-scatter.2.cloned.1.call-done) | copy-start | bytes 4915204
  253.8 18.7 %collective-permute-start.2 = (bf16[1,2,256,640]{3,2,1,0:T(8,128)(2,1)S(1)}, bf16[1,2,256,640]{3,2,1,0:T(8,128)(2,1)S(1)}, u32[]{:S(2)}, u32[]{:S(2)}) collective-permute-start(bf16[1,2,256,640]{3,2,1,0:T(8,128)(2,1)S(1)} %slice.128), channel_id=1, source_target_pairs={{0,4},{4,8},{8,12},{1,5},{5,9},{9,13},{2,6},{6,10},{10,14},{3,7},{... | collective-permute-start | bytes 1966088 | tf_op jit(solution)/shard_map/ppermute | solution.py:12
  272.7 12.2 %collective-permute-start.3 = (bf16[1,2,384,256]{3,2,1,0:T(8,128)(2,1)S(1)}, bf16[1,2,384,256]{3,2,1,0:T(8,128)(2,1)S(1)}, u32[]{:S(2)}, u32[]{:S(2)}) collective-permute-start(bf16[1,2,384,256]{3,2,1,0:T(8,128)(2,1)S(1)} %fusion.339), channel_id=1, source_target_pairs={{0,2},{1,3},{4,6},{5,7},{8,10},{9,11},{12,14},{13,15},{16,18},{17,... | collective-permute-start | bytes 1179656 | tf_op jit(solution)/shard_map/ppermute | solution.py:12
Sparse Core Ops, SparseCore 0:
  239.8 12.7 reduce-scatter.1
